TPU v7x, 32 devices: a whole 2x2x4 slice. The times are simulated.
32 devices in a mesh: chan: 4 (over y, core), inp: 8 (over z, x).
Axes of the slice: x: 2, y: 2, z: 4, core: 2. Of those that a mesh axis runs over, the one named last changes fastest.
Arguments:
- voltages: bfloat16 [1024, 131072], P('inp', 'chan'), may hold values from -64 to 64
- tile_table: int32 [40, 2], replicated, may hold values from -1 to 7, as said below
Outputs:
- coherence: float32 [512, 40, 128, 256], P('chan', 'inp')
Inputs may be any that keep to these rules, and one draw needn't show every extreme that they name: `tile_table`: rows 5 d to 5 d + 4 are the slots whose tiles the device at index d along inp outputs. Every pair (a, b) with 0 <= a <= b < 8 stands in exactly one row, and every other row is (-1, -1); the pairs are spread over the rows in any order.
All inputs are finite; a program needn't handle non-finite values.
Results may differ from a plain program's by a relative error of at most 0.0058.
Values may be sent and summed in bfloat16 or wider, within the bound.
A program may use at most 256 MiB of HBM per device.

v0:
```python
import math

import jax
import jax.numpy as jnp
from jax import lax
from jax.sharding import PartitionSpec as P

L = 2048
NCH = 512
TAPS = 4


def passed_along(array, axis, by):
    devices = lax.axis_size(axis)
    pairs = [(i, i + by) for i in range(devices) if 0 <= i + by < devices]
    return lax.ppermute(array, axis, pairs)


def filter_window():
    positions = jnp.arange(TAPS * L, dtype=jnp.float32)
    shape_sinc = jnp.sinc((positions - TAPS * L / 2.0) / L)
    tapering = 0.5 - 0.5 * jnp.cos(2.0 * math.pi * positions / (TAPS * L))
    return (shape_sinc * tapering).reshape(TAPS, L)


def transform_table():
    samples = jnp.arange(L, dtype=jnp.int32)[:, None]
    channels = jnp.arange(NCH, dtype=jnp.int32)[None, :]
    phases = samples * channels % L
    angles = phases.astype(jnp.float32) * (2.0 * math.pi / L)
    return (
        jnp.stack([jnp.cos(angles), -jnp.sin(angles)], axis=2)
        .reshape(L, 2 * NCH)
        .astype(jnp.bfloat16)
    )


def rotate_parts(rows):
    half_width = rows.shape[-1] // 2
    return jnp.concatenate([-rows[..., half_width:], rows[..., :half_width]], axis=-1)


def arrange(turned):
    input_count, frame_total, column_count = turned.shape
    return (
        turned.reshape(input_count, frame_total, column_count // 2, 2)
        .transpose(2, 0, 3, 1)
        .reshape(column_count // 2, input_count, 2 * frame_total)
    )


def channelize(voltages):
    block_width, local_len = voltages.shape
    local_frames = local_len // L
    blocks = voltages.reshape(block_width, local_frames, L)
    following = passed_along(blocks[:, : TAPS - 1, :], "chan", -1)
    extended = jnp.concatenate([blocks, following], axis=1)
    window = filter_window()
    filtered = jnp.zeros((block_width, local_frames, L), jnp.float32)
    for tap_index in range(TAPS):
        filtered = (
            filtered
            + extended[:, tap_index : tap_index + local_frames, :].astype(jnp.float32)
            * window[tap_index]
        )
    filtered = filtered.astype(jnp.bfloat16).reshape(block_width * local_frames, L)
    spectra = jnp.dot(filtered, transform_table(), preferred_element_type=jnp.float32).astype(
        jnp.bfloat16
    )
    return spectra.reshape(block_width, local_frames, 2 * NCH)


def make_tile(everything, autopower, row_block, col_block, block_width, frame_total):
    present = (row_block >= 0).astype(jnp.float32)
    first = jnp.maximum(row_block, 0)
    second = jnp.maximum(col_block, 0)
    left_rows = lax.dynamic_slice_in_dim(everything, first * block_width, block_width, 1)
    right_rows = lax.dynamic_slice_in_dim(everything, second * block_width, block_width, 1)
    partner = jnp.concatenate([right_rows, rotate_parts(right_rows)], axis=1)
    product = jnp.einsum("cif,cjf->cij", left_rows, partner, preferred_element_type=jnp.float32)
    power_left = lax.dynamic_slice_in_dim(autopower, first * block_width, block_width, 1)
    power_right = lax.dynamic_slice_in_dim(autopower, second * block_width, block_width, 1)
    inverse = present / (frame_total * jnp.sqrt(power_left[:, :, None] * power_right[:, None, :]))
    return product * jnp.concatenate([inverse, inverse], axis=2)


def on_device(voltages, tile_table):
    block_width = voltages.shape[0]
    spectra = channelize(voltages)
    turned = lax.all_to_all(spectra, "chan", split_axis=2, concat_axis=1, tiled=True)
    own = arrange(turned)
    everything = lax.all_gather(own, "inp", axis=1, tiled=True)
    frame_total = everything.shape[2] // 2
    autopower = jnp.sum(jnp.square(everything.astype(jnp.float32)), axis=2) / frame_total + 1e-06
    slot_total = tile_table.shape[0] // lax.axis_size("inp")
    device_index = lax.axis_index("inp")
    slot_rows = lax.dynamic_slice_in_dim(tile_table, device_index * slot_total, slot_total, 0)
    outputs = jnp.zeros(
        (everything.shape[0], slot_total, block_width, 2 * block_width), jnp.float32
    )

    def place(slot_index, current):
        tile_out = make_tile(
            everything,
            autopower,
            slot_rows[slot_index, 0],
            slot_rows[slot_index, 1],
            block_width,
            frame_total,
        )
        return lax.dynamic_update_index_in_dim(current, tile_out, slot_index, 1)

    return lax.fori_loop(0, slot_total, place, outputs)


def solution(mesh):
    placed = (P("inp", "chan"), P())
    return jax.shard_map(
        on_device,
        mesh=mesh,
        in_specs=placed,
        out_specs=P("chan", "inp", None, None),
        check_vma=False,
    )
```

profile of v0, /device:TPU:0, one launch (start us, length us, event | category | flops | bytes accessed | tf_op | source)
XLA Modules:
  0.0 1064.4 jit_solution(10083409122498932907)
XLA Ops:
  6.5 11.9 %copy.24 = bf16[128,32768]{0,1:T(8,128)(2,1)} copy(bf16[128,32768]{1,0:T(8,128)(2,1)} %param.4) | data formatting | bytes 16777216 | tf_op args[0]
  18.4 1.5 slice.51
  20.0 0.7 copy.25
  20.7 1.3 collective-permute-start
  22.0 17.1 %negate_convert_fusion = (bf16[2048,512,1]{1,0,2:T(8,128)(2,1)S(1)}, bf16[2048,512,1]{1,0,2:T(8,128)(2,1)S(1)}) fusion(), kind=kLoop, calls=%fused_computation.35 | loop fusion | flops 17825792 | bytes 4194304 | tf_op jit(solution)/shard_map/convert.2
  39.1 2.3 pad_maximum_fusion.1
  41.4 11.3 %copy.28 = bf16[2048,512,2]{0,2,1:T(2,128)(2,1)} copy(bf16[2048,512,2]{1,0,2:T(8,128)(2,1)} %pad_maximum_fusion.1) | data formatting | bytes 8388608 | tf_op jit(solution)/shard_map/stack | solution.py:32
  52.7 7.2 convert_element_type.68
  60.1 1.9 copy.26
  62.1 16.3 %add_convert_fusion = bf16[128,16,2048]{0,2,1:T(8,128)(2,1)} fusion(bf16[128,16,2048]{0,2,1:T(8,128)(2,1)} %bitcast.33, bf16[128,3,2048]{0,2,1:T(8,128)(2,1)S(1)} %copy.26, f32[2048]{0:T(1024)S(1)} %get-tuple-element.142, f32[2048]{0:T(1024)S(1)} %get-tuple-element.143, f32[2048]{0:T(1024)S(1)} %get-tuple-element.144, f32[2048]{0:T(1024)S(1)} %get-tuple-element.141), kind=kLoop, calls=%fused_computation.20 | loop fusion | flops 62914560 | bytes 18382848 | tf_op jit(solution)/shard_map/convert_element_type | solution.py:66
  78.4 12.5 %copy.27 = bf16[128,16,2048]{2,1,0:T(8,128)(2,1)} copy(bf16[128,16,2048]{0,2,1:T(8,128)(2,1)} %add_convert_fusion) | data formatting | bytes 16777216 | tf_op jit(solution)/shard_map/convert_element_type | solution.py:66
  90.8 13.9 %convolution_convert_fusion = bf16[2048,1024]{1,0:T(8,128)(2,1)} fusion(bf16[2048,2048]{1,0:T(8,128)(2,1)} %bitcast.36, bf16[2048,1024]{0,1:T(8,128)(2,1)} %convert_element_type.68), kind=kOutput, calls=%fused_computation.40 | convolution fusion | flops 8592031744 | bytes 16777216 | tf_op jit(solution)/shard_map/dot_general | solution.py:67
  104.7 7.2 copy.29
  111.9 54.5 %all_to_all.15 = bf16[128,16,1024]{0,1,2:T(8,128)(2,1)S(1)} all-to-all(bf16[128,16,1024]{0,1,2:T(8,128)(2,1)} %copy.29), channel_id=1, replica_groups=mesh['chan'=4,'inp'=8] {'chan'}, dimensions={2} | all-to-all | bytes 8388608 | tf_op jit(solution)/shard_map/all_to_all | solution.py:90
  166.5 3.3 copy.31
  169.9 639.2 %all-gather.2.cloned.1.call-done = bf16[128,1024,128]{1,2,0:T(8,128)(2,1)} async-done(((bf16[128,128,128]{1,2,0:T(8,128)(2,1)}), bf16[128,1024,128]{1,2,0:T(8,128)(2,1)}) %all-gather.2.cloned.1.call-update) | async-done | bytes 33554448 | tf_op jit(solution)/shard_map/all_gather | solution.py:92
  809.1 11.4 %multiply_reduce_fusion = f32[128,1024]{1,0:T(8,128)S(1)} fusion(bf16[128,1024,128]{1,2,0:T(8,128)(2,1)} %all-gather.2.cloned.1.call-done), kind=kLoop, calls=%fused_computation.19 | loop fusion | flops 50200576 | bytes 34078720 | tf_op jit(solution)/shard_map/reduce_sum | solution.py:94
  820.5 40.7 %copy.32 = bf16[128,1024,128]{2,1,0:T(8,128)(2,1)} copy(bf16[128,1024,128]{1,2,0:T(8,128)(2,1)} %all-gather.2.cloned.1.call-done) | data formatting | bytes 67108864 | tf_op jit(solution)/shard_map/while | solution.py:113
  861.2 195.6 %while.13 = (s32[]{:T(128)}, f32[128,5,128,256]{3,2,1,0:T(8,128)}, s32[5,2]{0,1:T(2,128)S(1)}, bf16[128,1024,128]{2,1,0:T(8,128)(2,1)}, f32[128,1024]{1,0:T(8,12...) while((s32[]{:T(128)}, f32[128,5,128,256]{3,2,1,0:T(8,128)}, ...), condition=%wide.region_2.3_spmd, body=%wide.region_1.2_spmd.sunk | while | flops 1116733440 | bytes 101057344 | solution.py:113
  861.2 0.6 constant_dynamic-slice_fusion.10
  863.7 7.8 multiply_divide_fusion.2
  871.6 10.9 %dynamic-slice_negate_fusion.2 = (bf16[128,128,64]{2,1,0:T(8,128)(2,1)}, bf16[128,128,64]{2,1,0:T(8,128)(2,1)}) fusion(bf16[128,1024,128]{2,1,0:T(8,128)(2,1)} %get-tuple-element.215, s32[]{:T(128)S(6)} %select_n.191, s32[]{:T(128)S(6)} %add.289), kind=kLoop, calls=%fused_computation.9.clone.1 | loop fusion | flops 3145728 | bytes 8388616 | tf_op jit(solution)/shard_map/while/body/eval_jaxpr/neg | solution.py:40
  882.5 5.1 constant_dynamic-slice_fusion.12
  887.6 1.1 copy-done.2
  888.7 11.7 %fusion.54 = f32[128,5,128,256]{3,2,1,0:T(8,128)} fusion(f32[128,5,128,256]{3,2,1,0:T(8,128)} %get-tuple-element.202, s32[]{:T(128)} %get-tuple-element.201, f32[128,128,128]{2,1,0:T(8,128)S(1)} %copy-done.2, bf16[128,128,64]{2,1,0:T(8,128)(2,1)} %get-tuple-element.188, bf16[128,128,64]{2,1,0:T(8,128)(2,1)} %get-tuple-element.189, ...), kind=kOutput, calls=%fused_computation.2.clone.1 | convolution fusion | flops 1107296256 | bytes 41943556 | tf_op jit(solution)/shard_map/while/body/eval_jaxpr/cif,cjf->cij/dot_general | solution.py:80
  902.8 7.8 multiply_divide_fusion.2
  910.7 10.9 %dynamic-slice_negate_fusion.2 = (bf16[128,128,64]{2,1,0:T(8,128)(2,1)}, bf16[128,128,64]{2,1,0:T(8,128)(2,1)}) fusion(bf16[128,1024,128]{2,1,0:T(8,128)(2,1)} %get-tuple-element.215, s32[]{:T(128)S(6)} %select_n.191, s32[]{:T(128)S(6)} %add.289), kind=kLoop, calls=%fused_computation.9.clone.1 | loop fusion | flops 3145728 | bytes 8388616 | tf_op jit(solution)/shard_map/while/body/eval_jaxpr/neg | solution.py:40
  921.6 5.1 constant_dynamic-slice_fusion.12
  926.7 1.1 copy-done.2
  927.8 11.7 %fusion.54 = f32[128,5,128,256]{3,2,1,0:T(8,128)} fusion(f32[128,5,128,256]{3,2,1,0:T(8,128)} %get-tuple-element.202, s32[]{:T(128)} %get-tuple-element.201, f32[128,128,128]{2,1,0:T(8,128)S(1)} %copy-done.2, bf16[128,128,64]{2,1,0:T(8,128)(2,1)} %get-tuple-element.188, bf16[128,128,64]{2,1,0:T(8,128)(2,1)} %get-tuple-element.189, ...), kind=kOutput, calls=%fused_computation.2.clone.1 | convolution fusion | flops 1107296256 | bytes 41943556 | tf_op jit(solution)/shard_map/while/body/eval_jaxpr/cif,cjf->cij/dot_general | solution.py:80
  939.5 0.6 constant_dynamic-slice_fusion.10
  942.0 7.8 multiply_divide_fusion.2
  949.8 10.9 %dynamic-slice_negate_fusion.2 = (bf16[128,128,64]{2,1,0:T(8,128)(2,1)}, bf16[128,128,64]{2,1,0:T(8,128)(2,1)}) fusion(bf16[128,1024,128]{2,1,0:T(8,128)(2,1)} %get-tuple-element.215, s32[]{:T(128)S(6)} %select_n.191, s32[]{:T(128)S(6)} %add.289), kind=kLoop, calls=%fused_computation.9.clone.1 | loop fusion | flops 3145728 | bytes 8388616 | tf_op jit(solution)/shard_map/while/body/eval_jaxpr/neg | solution.py:40
  960.7 5.1 constant_dynamic-slice_fusion.12
  965.8 1.1 copy-done.2
  966.9 11.7 %fusion.54 = f32[128,5,128,256]{3,2,1,0:T(8,128)} fusion(f32[128,5,128,256]{3,2,1,0:T(8,128)} %get-tuple-element.202, s32[]{:T(128)} %get-tuple-element.201, f32[128,128,128]{2,1,0:T(8,128)S(1)} %copy-done.2, bf16[128,128,64]{2,1,0:T(8,128)(2,1)} %get-tuple-element.188, bf16[128,128,64]{2,1,0:T(8,128)(2,1)} %get-tuple-element.189, ...), kind=kOutput, calls=%fused_computation.2.clone.1 | convolution fusion | flops 1107296256 | bytes 41943556 | tf_op jit(solution)/shard_map/while/body/eval_jaxpr/cif,cjf->cij/dot_general | solution.py:80
  981.1 7.8 multiply_divide_fusion.2
  988.9 10.9 %dynamic-slice_negate_fusion.2 = (bf16[128,128,64]{2,1,0:T(8,128)(2,1)}, bf16[128,128,64]{2,1,0:T(8,128)(2,1)}) fusion(bf16[128,1024,128]{2,1,0:T(8,128)(2,1)} %get-tuple-element.215, s32[]{:T(128)S(6)} %select_n.191, s32[]{:T(128)S(6)} %add.289), kind=kLoop, calls=%fused_computation.9.clone.1 | loop fusion | flops 3145728 | bytes 8388616 | tf_op jit(solution)/shard_map/while/body/eval_jaxpr/neg | solution.py:40
  999.8 5.1 constant_dynamic-slice_fusion.12
  1004.9 1.1 copy-done.2
  1006.0 11.7 %fusion.54 = f32[128,5,128,256]{3,2,1,0:T(8,128)} fusion(f32[128,5,128,256]{3,2,1,0:T(8,128)} %get-tuple-element.202, s32[]{:T(128)} %get-tuple-element.201, f32[128,128,128]{2,1,0:T(8,128)S(1)} %copy-done.2, bf16[128,128,64]{2,1,0:T(8,128)(2,1)} %get-tuple-element.188, bf16[128,128,64]{2,1,0:T(8,128)(2,1)} %get-tuple-element.189, ...), kind=kOutput, calls=%fused_computation.2.clone.1 | convolution fusion | flops 1107296256 | bytes 41943556 | tf_op jit(solution)/shard_map/while/body/eval_jaxpr/cif,cjf->cij/dot_general | solution.py:80
  1017.7 0.6 constant_dynamic-slice_fusion.10
  1020.2 7.8 multiply_divide_fusion.2
  1028.1 10.9 %dynamic-slice_negate_fusion.2 = (bf16[128,128,64]{2,1,0:T(8,128)(2,1)}, bf16[128,128,64]{2,1,0:T(8,128)(2,1)}) fusion(bf16[128,1024,128]{2,1,0:T(8,128)(2,1)} %get-tuple-element.215, s32[]{:T(128)S(6)} %select_n.191, s32[]{:T(128)S(6)} %add.289), kind=kLoop, calls=%fused_computation.9.clone.1 | loop fusion | flops 3145728 | bytes 8388616 | tf_op jit(solution)/shard_map/while/body/eval_jaxpr/neg | solution.py:40
  1039.0 5.1 constant_dynamic-slice_fusion.12
  1044.0 1.1 copy-done.2
  1045.1 11.7 %fusion.54 = f32[128,5,128,256]{3,2,1,0:T(8,128)} fusion(f32[128,5,128,256]{3,2,1,0:T(8,128)} %get-tuple-element.202, s32[]{:T(128)} %get-tuple-element.201, f32[128,128,128]{2,1,0:T(8,128)S(1)} %copy-done.2, bf16[128,128,64]{2,1,0:T(8,128)(2,1)} %get-tuple-element.188, bf16[128,128,64]{2,1,0:T(8,128)(2,1)} %get-tuple-element.189, ...), kind=kOutput, calls=%fused_computation.2.clone.1 | convolution fusion | flops 1107296256 | bytes 41943556 | tf_op jit(solution)/shard_map/while/body/eval_jaxpr/cif,cjf->cij/dot_general | solution.py:80
  1056.8 0.7 copy-done.1
  (23 shorter events, 1.7 us)
Async XLA Ops:
  6.5 163.2 %copy-start = (s32[40,2]{0,1:T(2,128)S(1)}, s32[40,2]{0,1:T(2,128)}, u32[]{:S(2)}) copy-start(s32[40,2]{0,1:T(2,128)} %param.5) | copy-start | bytes 964
  6.5 802.6 %all-gather.2.cloned.1.call-start = ((), (), s32[]{:S(2)}) async-start(), calls=%async_computation.1 | async-start | bytes 37748736 | tf_op jit(solution)/shard_map/all_gather | solution.py:92
  20.7 39.5 %collective-permute-start = (bf16[128,3,2048]{2,0,1:T(8,128)(2,1)S(1)}, bf16[128,3,2048]{2,0,1:T(8,128)(2,1)}, u32[]{:S(2)}, u32[]{:S(2)}) collective-permute-start(bf16[128,3,2048]{2,0,1:T(8,128)(2,1)S(1)} %copy.25), channel_id=1, source_target_pairs={{8,0},{16,8},{24,16},{9,1},{17,9},{25,17},{10,2},{18,10},{26,18},{... | collective-permute-start | bytes 4718600 | tf_op jit(solution)/shard_map/ppermute | solution.py:16
  882.5 6.2 copy-start.2
  921.6 6.2 copy-start.2
  960.7 6.2 copy-start.2
  999.8 6.2 copy-start.2
  1039.0 6.2 copy-start.2
  1056.8 0.7 copy-start.1
Sparse Core Ops, SparseCore 0:
  169.9 639.1 all-gather.1
where the time goes:
time: 1070 us; the launch traced here: 1060 us
  waiting for transfers between devices  639 us (60%)
  other arithmetic  141 us (13%)
  local copies, waits for them, and re-layouts  133 us (12%)
  matrix products  72.3 us (7%)
  blocking collectives  54.5 us (5%)
  between operations  13.5 us (1%)
    all_gather x1, waiting for transfers between devices, on_device(): everything = lax.all_gather(own, 'inp', axis=1, tiled=True)  639 us
    dot_general x5, matrix products, make_tile(): jnp.einsum('cif,cjf->cij', left_rows, partner, preferred_element_type=jnp...  58.5 us
    neg x5, other arithmetic, rotate_parts(): -rows[..., half_width:]  54.6 us
    all_to_all x1, blocking collectives, on_device(): lax.all_to_all(spectra, 'chan', split_axis=2, concat_axis=1, tiled=True)  54.5 us
    while x1, local copies, waits for them, and re-layouts, on_device(): return lax.fori_loop(0, slot_total, place, outputs)  40.7 us
    div x5, other arithmetic, make_tile(): present / (frame_total * jnp.sqrt(power_left[:, :, None] * power_right[:,...  39.2 us
    dynamic_slice x5, local copies, waits for them, and re-layouts, make_tile(): lax.dynamic_slice_in_dim(everything, second * block_width, block_width, 1)  25.4 us
  transfers between devices with their start and end apart: 2, of which 1 were waited for; matrix products, arithmetic and copies ran while one was open for 4% of the time, Pallas kernels for 0%

commit v1 on v0

v1 whole, which is shorter than its diff:
```python
import functools
import math

import jax
import jax.numpy as jnp
from jax import lax
from jax.experimental import pallas as pl
from jax.experimental.pallas import tpu as pltpu
from jax.sharding import PartitionSpec as P

L = 2048
NCH = 512
TAPS = 4
FINE = 64
MESH = pl.DeviceIdType.MESH


def passed_along(array, axis, by):
    devices = lax.axis_size(axis)
    pairs = [(i, i + by) for i in range(devices) if 0 <= i + by < devices]
    return lax.ppermute(array, axis, pairs)


def filter_window():
    positions = jnp.arange(TAPS * L, dtype=jnp.float32)
    shape_sinc = jnp.sinc((positions - TAPS * L / 2.0) / L)
    tapering = 0.5 - 0.5 * jnp.cos(2.0 * math.pi * positions / (TAPS * L))
    return (shape_sinc * tapering).reshape(TAPS, L)


def turn_angles(samples):
    channels = jnp.arange(NCH, dtype=jnp.int32)[None, :]
    phases = samples[:, None] * channels % L
    angles = phases.astype(jnp.float32) * (2.0 * math.pi / L)
    return jnp.cos(angles), jnp.sin(angles)


def transform_table(groups):
    coarse_cos, coarse_sin = turn_angles(jnp.arange(L // FINE, dtype=jnp.int32) * FINE)
    fine_cos, fine_sin = turn_angles(jnp.arange(FINE, dtype=jnp.int32))
    coarse_cos, coarse_sin = coarse_cos[:, None, :], coarse_sin[:, None, :]
    fine_cos, fine_sin = fine_cos[None], fine_sin[None]
    real = (coarse_cos * fine_cos - coarse_sin * fine_sin).reshape(L, groups, 1, -1)
    imag = -(coarse_sin * fine_cos + coarse_cos * fine_sin).reshape(L, groups, 1, -1)
    return (
        jnp.concatenate([real.astype(jnp.bfloat16), imag.astype(jnp.bfloat16)], axis=2)
        .reshape(L, 2 * NCH)
    )


def channelize(voltages, groups):
    block_width, local_len = voltages.shape
    local_frames = local_len // L
    following = passed_along(voltages[:, : (TAPS - 1) * L], "chan", -1)
    extended = jnp.concatenate([voltages, following], axis=1).reshape(
        block_width, local_frames + TAPS - 1, L
    )
    window = filter_window()
    filtered = jnp.zeros((block_width, local_frames, L), jnp.float32)
    for tap_index in range(TAPS):
        filtered = (
            filtered
            + extended[:, tap_index : tap_index + local_frames, :].astype(jnp.float32)
            * window[tap_index]
        )
    filtered = filtered.astype(jnp.bfloat16).reshape(block_width * local_frames, L)
    spectra = jnp.dot(
        filtered, transform_table(groups), preferred_element_type=jnp.float32
    ).astype(jnp.bfloat16)
    return spectra.reshape(block_width, local_frames, 2 * NCH)


def arrange(turned):
    input_count, frame_total, column_count = turned.shape
    rows = (
        turned.reshape(input_count, frame_total, 2, column_count // 2)
        .transpose(3, 0, 2, 1)
        .reshape(column_count // 2, input_count, 2 * frame_total)
    ).astype(jnp.float32)
    autopower = jnp.sum(jnp.square(rows), axis=2, keepdims=True) / frame_total + 1e-06
    return (rows / (math.sqrt(frame_total) * jnp.sqrt(autopower))).astype(jnp.bfloat16)


def gather_kernel(sizes, own_ref, all_ref, stage, send_line, send_cross, recv_sem, local_sem):
    rows, columns, chunks, crossed = sizes
    step = own_ref.shape[0] // chunks
    me = lax.axis_index("inp")
    z, x = lax.div(me, columns), lax.rem(me, columns)
    up = ("up", 0, z < rows - 1, me + columns)
    down = ("down", 1, z > 0, me - columns)
    right = ("right", 2, x < columns - 1, me + 1)
    left = ("left", 3, x > 0, me - 1)
    along_z, along_x = (up, down), (right, left)

    barrier = pltpu.get_barrier_semaphore()
    expected = jnp.int32(0)
    for _, _, exists, target in along_z + along_x:
        expected = expected + exists.astype(jnp.int32)

        @pl.when(exists)
        def _(target=target):
            pl.semaphore_signal(barrier, inc=1, device_id={"inp": target}, device_id_type=MESH)

    pl.semaphore_wait(barrier, expected)

    def part(ref, chunk):
        return ref.at[pl.ds(chunk * step, step)]

    def copy(source, block, chunk, way, sems):
        return pltpu.make_async_remote_copy(
            src_ref=part(source, chunk),
            dst_ref=part(all_ref.at[block], chunk),
            send_sem=sems.at[way[1], block],
            recv_sem=recv_sem.at[block, chunk],
            device_id={"inp": way[3]},
            device_id_type=MESH,
        )

    def send(source, block, chunk, ways, sems):
        for way in ways:

            @pl.when(way[2])
            def _(way=way):
                copy(source, block, chunk, way, sems).start()

    def pass_on(block, chunk, exists, ways, sems, origin):
        @pl.when(exists)
        def _():
            copy(all_ref.at[block], block, chunk, origin, sems).wait_recv()
            send(all_ref.at[block], block, chunk, ways, sems)

    def over(first, last, body):
        def one(chunk, carry):
            body(chunk)
            return carry

        lax.fori_loop(first, last, one, jnp.int32(0))

    over(0, crossed, lambda c: send(own_ref, me, c, along_x + along_z, send_cross))
    over(crossed, chunks, lambda c: send(own_ref, me, c, along_z + along_x, send_line))
    load = pltpu.make_async_copy(own_ref, stage, local_sem.at[0])
    load.start()
    load.wait()
    store = pltpu.make_async_copy(stage, all_ref.at[me], local_sem.at[1])
    store.start()

    for away in range(1, columns):
        over(
            0,
            crossed,
            lambda c: (
                pass_on(me - away, c, x >= away, (right,) + along_z, send_cross, left),
                pass_on(me + away, c, x + away < columns, (left,) + along_z, send_cross, right),
            ),
        )
    for away in range(1, rows):
        below, above = z >= away, z + away < rows
        over(
            crossed,
            chunks,
            lambda c: (
                pass_on(me - away * columns, c, below, along_x + (up,), send_line, down),
                pass_on(me + away * columns, c, above, along_x + (down,), send_line, up),
            ),
        )
        for column in range(columns):
            low = (z - away) * columns + column
            high = (z + away) * columns + column
            over(
                0,
                crossed,
                lambda c: (
                    pass_on(low, c, below, (up,), send_cross, down),
                    pass_on(high, c, above, (down,), send_cross, up),
                ),
            )
    for away in range(1, columns):
        for row in range(rows):
            before = row * columns + x - away
            after = row * columns + x + away
            over(
                crossed,
                chunks,
                lambda c: (
                    pass_on(before, c, x >= away, (right,), send_line, left),
                    pass_on(after, c, x + away < columns, (left,), send_line, right),
                ),
            )

    def drain(block, way, cond, sems, first, count):
        @pl.when(jnp.logical_and(cond, way[2]))
        def _():
            whole = all_ref.at[block, pl.ds(first * step, count * step)]
            pltpu.make_async_remote_copy(
                src_ref=whole,
                dst_ref=whole,
                send_sem=sems.at[way[1], block],
                recv_sem=recv_sem.at[block, 0],
                device_id={"inp": way[3]},
                device_id_type=MESH,
            ).wait_send()

    for row in range(rows):
        for column in range(columns):
            block = row * columns + column
            plain, turned = chunks - crossed, crossed
            here = x == column
            drain(block, up, jnp.logical_and(here, z >= row), send_line, crossed, plain)
            drain(block, down, jnp.logical_and(here, z <= row), send_line, crossed, plain)
            drain(block, right, x >= column, send_line, crossed, plain)
            drain(block, left, x <= column, send_line, crossed, plain)
            if turned:
                same = z == row
                drain(block, up, z >= row, send_cross, 0, turned)
                drain(block, down, z <= row, send_cross, 0, turned)
                drain(block, right, jnp.logical_and(same, x >= column), send_cross, 0, turned)
                drain(block, left, jnp.logical_and(same, x <= column), send_cross, 0, turned)
    store.wait()


def gather(own):
    devices = lax.axis_size("inp")
    columns = 1 << (int(math.log2(devices)) // 2)
    rows = devices // columns
    chunks = 8
    crossed = 1
    return pl.pallas_call(
        functools.partial(gather_kernel, (rows, columns, chunks, crossed)),
        out_shape=jax.ShapeDtypeStruct((devices,) + own.shape, own.dtype),
        in_specs=[pl.BlockSpec(memory_space=pl.ANY)],
        out_specs=pl.BlockSpec(memory_space=pl.ANY),
        scratch_shapes=[
            pltpu.VMEM(own.shape, own.dtype),
            pltpu.SemaphoreType.DMA((4, devices)),
            pltpu.SemaphoreType.DMA((4, devices)),
            pltpu.SemaphoreType.DMA((devices, chunks)),
            pltpu.SemaphoreType.DMA((2,)),
        ],
        compiler_params=pltpu.CompilerParams(collective_id=0, has_side_effects=True),
        name="gather",
    )(own)


def tile_kernel(slots, table_ref, all_ref, out_ref):
    def one(channel, carry):
        for slot in range(slots):
            first, second = table_ref[slot, 0], table_ref[slot, 1]
            present = first >= 0

            @pl.when(present)
            def _(slot=slot, first=first, second=second):
                left = all_ref[first, channel]
                right = all_ref[second, channel]
                half = right.shape[1] // 2
                turned = jnp.concatenate([-right[:, half:], right[:, :half]], axis=1)
                partner = jnp.concatenate([right, turned], axis=0)
                out_ref[channel, slot] = lax.dot_general(
                    left,
                    partner,
                    (((1,), (1,)), ((), ())),
                    preferred_element_type=jnp.float32,
                )

            @pl.when(jnp.logical_not(present))
            def _(slot=slot):
                out_ref[channel, slot] = jnp.zeros(out_ref.shape[2:], jnp.float32)

        return carry

    lax.fori_loop(0, all_ref.shape[1], one, jnp.int32(0), unroll=2)


def make_tiles(everything, slot_rows):
    devices, channel_count, block_width, depth = everything.shape
    slots = slot_rows.shape[0]
    group = 8
    return pl.pallas_call(
        functools.partial(tile_kernel, slots),
        out_shape=jax.ShapeDtypeStruct(
            (channel_count, slots, block_width, 2 * block_width), jnp.float32
        ),
        grid_spec=pltpu.PrefetchScalarGridSpec(
            num_scalar_prefetch=1,
            grid=(channel_count // group,),
            in_specs=[
                pl.BlockSpec((devices, group, block_width, depth), lambda c, t: (0, c, 0, 0))
            ],
            out_specs=pl.BlockSpec(
                (group, slots, block_width, 2 * block_width), lambda c, t: (c, 0, 0, 0)
            ),
        ),
        compiler_params=pltpu.CompilerParams(vmem_limit_bytes=56 << 20),
        name="tiles",
    )(slot_rows, everything)


def on_device(voltages, tile_table):
    spectra = channelize(voltages, lax.axis_size("chan"))
    turned = lax.all_to_all(spectra, "chan", split_axis=2, concat_axis=1, tiled=True)
    everything = gather(arrange(turned))
    slot_total = tile_table.shape[0] // lax.axis_size("inp")
    slot_rows = lax.dynamic_slice_in_dim(
        tile_table, lax.axis_index("inp") * slot_total, slot_total, 0
    )
    return make_tiles(everything, slot_rows)


def solution(mesh):
    placed = (P("inp", "chan"), P())
    return jax.shard_map(
        on_device,
        mesh=mesh,
        in_specs=placed,
        out_specs=P("chan", "inp", None, None),
        check_vma=False,
    )
```

time: 1070 us -> 670 us (0.63)
  the two profiles are of different devices: /device:TPU:0 before, /device:TPU:9 now
where the time goes in v1:
time: 670 us; the launch traced here: 669 us
  Pallas kernels  488 us (73%)
  local copies, waits for them, and re-layouts  69.9 us (10%)
  waiting for transfers between devices  46.8 us (7%)
  other arithmetic  42.6 us (6%)
  matrix products  13.9 us (2%)
  starting transfers between devices  7.62 us (1%)
    pallas_call x1, Pallas kernels, gather(): pl.pallas_call(functools.partial(gather_kernel, (rows, columns, chunks, c...  331 us
    pallas_call x1, Pallas kernels, make_tiles(): pl.pallas_call(functools.partial(tile_kernel, slots), out_shape=jax.Shape...  157 us
    all_to_all x1, waiting for transfers between devices, on_device(): lax.all_to_all(spectra, 'chan', split_axis=2, concat_axis=1, tiled=True)  46.8 us
    convert_element_type x3, local copies, waits for them, and re-layouts, arrange(): rows = turned.reshape(input_count, frame_total, 2, column_count // 2).tra...  21.2 us
    dot_general x1, matrix products, channelize(): jnp.dot(filtered, transform_table(groups), preferred_element_type=jnp.flo...  13.9 us
  transfers between devices with their start and end apart: 2, of which 1 were waited for; matrix products, arithmetic and copies ran while one was open for 4% of the time, Pallas kernels for 0%

profile of v1, /device:TPU:9, one launch (start us, length us, event | category | flops | bytes accessed | tf_op | source)
XLA Modules:
  0.0 668.5 jit_solution(6517350703763397905)
XLA Ops:
  0.0 0.0 copy-start
  0.0 11.9 %copy.20 = bf16[128,32768]{0,1:T(8,128)(2,1)} copy(bf16[128,32768]{1,0:T(8,128)(2,1)} %param.2) | data formatting | bytes 16777216 | tf_op args[0]
  11.9 2.7 slice.40
  14.6 2.6 collective-permute-start
  17.2 0.5 fusion.10
  17.7 0.3 fusion.44
  18.1 2.8 subtract_convert_fusion
  20.9 4.0 convert_element_type.107
  24.9 2.1 convert_element_type.109
  26.9 6.2 pad_maximum_fusion.1
  33.1 7.5 %copy.22 = bf16[2048,4,2,128]{0,3,2,1:T(8,128)(2,1)} copy(bf16[2048,4,2,128]{3,1,0,2:T(4,128)(2,1)} %pad_maximum_fusion.1) | data formatting | bytes 8388608 | tf_op jit(solution)/shard_map/concatenate | solution.py:46
  40.7 0.2 fusion.19
  40.9 0.0 collective-permute-done
  40.9 8.4 %pad_maximum_fusion = bf16[128,38912]{0,1:T(8,128)(2,1)S(1)} fusion(bf16[128,6144]{0,1:T(8,128)(2,1)} %collective-permute-done, bf16[128,32768]{0,1:T(8,128)(2,1)} %copy.20), kind=kLoop, calls=%fused_computation.3 | loop fusion | flops 19922944 | bytes 19922944 | tf_op jit(solution)/shard_map/concatenate | solution.py:55
  49.2 9.5 %add_convert_fusion = bf16[128,16,2048]{0,2,1:T(8,128)(2,1)} fusion(bf16[128,19,2048]{0,2,1:T(8,128)(2,1)S(1)} %bitcast.18, f32[2048]{0:T(1024)S(1)} %get-tuple-element.10, f32[2048]{0:T(1024)S(1)} %get-tuple-element.11, f32[2048]{0:T(1024)S(1)} %get-tuple-element.12, f32[2048]{0:T(1024)S(1)} %get-tuple-element.9), kind=kLoop, calls=%fused_computation | loop fusion | flops 50331648 | bytes 41975808 | tf_op jit(solution)/shard_map/convert_element_type | solution.py:66
  58.8 12.5 %copy.21 = bf16[128,16,2048]{2,1,0:T(8,128)(2,1)} copy(bf16[128,16,2048]{0,2,1:T(8,128)(2,1)} %add_convert_fusion) | data formatting | bytes 16777216 | tf_op jit(solution)/shard_map/convert_element_type | solution.py:66
  71.3 13.9 %convolution_convert_fusion = bf16[2048,1024]{1,0:T(8,128)(2,1)} fusion(bf16[2048,2048]{1,0:T(8,128)(2,1)} %bitcast.22, bf16[2048,1024]{0,1:T(8,128)(2,1)} %bitcast.23), kind=kOutput, calls=%fused_computation.9 | convolution fusion | flops 8592031744 | bytes 16777216 | tf_op jit(solution)/shard_map/dot_general | solution.py:67
  85.1 7.3 %copy.23 = bf16[128,16,1024]{0,1,2:T(8,128)(2,1)} copy(bf16[128,16,1024]{2,1,0:T(8,128)(2,1)} %bitcast.24) | data formatting | bytes 8388608 | tf_op jit(solution)/shard_map/reshape | solution.py:70
  92.4 5.0 all-to-all-start
  97.5 0.0 copy-done
  97.5 0.1 constant_dynamic-slice_fusion
  97.6 0.7 copy.28.table_ref
  98.3 46.8 %all-to-all-done = bf16[128,16,1024]{0,1,2:T(8,128)(2,1)} async-done(((bf16[128,16,1024]{0,1,2:T(8,128)(2,1)}), bf16[128,16,1024]{0,1,2:T(8,128)(2,1)}, u32[]{:S(2)}, u32[]{:S(2)}) %all-to-all-start) | async-done | bytes 4194336 | tf_op jit(solution)/shard_map/all_to_all | solution.py:299
  145.1 6.9 %fusion.45 = (bf16[128,16,1024]{0,2,1:T(8,128)(2,1)S(1)}, f32[128,4,16,256]{0,3,1,2:T(8,128)}) fusion(bf16[128,16,1024]{0,1,2:T(8,128)(2,1)} %all-to-all-done), kind=kLoop, calls=%fused_computation.71 | loop fusion | flops 2097152 | bytes 16777216 | tf_op jit(solution)/shard_map/all_to_all | solution.py:299
  152.0 0.8 fusion
  152.9 3.9 copy.25
  156.8 8.3 %copy.26 = f32[128,128,2,64]{1,3,2,0:T(8,128)} copy(f32[128,128,2,64]{1,0,2,3:T(8,128)S(1)} %bitcast.19) | data formatting | bytes 16777216 | tf_op jit(solution)/shard_map/convert_element_type | solution.py:79
  165.1 9.0 %copy.27 = f32[128,128,128]{2,1,0:T(8,128)} copy(f32[128,128,128]{1,2,0:T(8,128)} %bitcast.20) | data formatting | bytes 16777216 | tf_op jit(solution)/shard_map/convert_element_type | solution.py:79
  174.1 6.8 %divide_convert_fusion.own_ref = bf16[128,128,128]{2,1,0:T(8,128)(2,1)} fusion(f32[128,128,128]{2,1,0:T(8,128)} %copy.27, f32[128,128]{1,0:T(8,128)S(1)} %multiply_bitcast_fusion), kind=kLoop, calls=%fused_computation.5 | loop fusion | flops 4194304 | bytes 12648448 | tf_op jit(solution)/shard_map/convert_element_type | solution.py:81
  180.9 330.9 %gather.1.all_ref = bf16[8,128,128,128]{3,2,1,0:T(8,128)(2,1)} custom-call(bf16[128,128,128]{2,1,0:T(8,128)(2,1)} %divide_convert_fusion.own_ref), custom_call_target="tpu_custom_call" | custom-call | tf_op jit(solution)/shard_map/gather/pallas_call | solution.py:227
  511.9 0.0 copy-start.1
  511.9 156.6 %tiles.1 = f32[128,5,128,256]{3,2,1,0:T(8,128)} custom-call(s32[5,2]{1,0:T(8,128)} %copy.28.table_ref, bf16[8,128,128,128]{3,2,1,0:T(8,128)(2,1)} %gather.1.all_ref), custom_call_target="tpu_custom_call" | custom-call | tf_op jit(solution)/shard_map/tiles/pallas_call | solution.py:277
  668.5 0.0 copy-done.1
  (4 shorter events, 0.0 us)
Async XLA Ops:
  0.0 97.5 %copy-start = (s32[40,2]{0,1:T(2,128)S(1)}, s32[40,2]{0,1:T(2,128)}, u32[]{:S(2)}) copy-start(s32[40,2]{0,1:T(2,128)} %param.3) | copy-start | bytes 964
  14.6 26.2 %collective-permute-start = (bf16[128,6144]{0,1:T(8,128)(2,1)}, bf16[128,6144]{0,1:T(8,128)(2,1)}, u32[]{:S(2)}, u32[]{:S(2)}) collective-permute-start(bf16[128,6144]{0,1:T(8,128)(2,1)} %slice.40), channel_id=1, source_target_pairs={{8,0},{16,8},{24,16},{9,1},{17,9},{25,17},{10,2},{18,10},{26,18},{... | collective-permute-start | bytes 4718600 | tf_op jit(solution)/shard_map/ppermute | solution.py:21
  92.4 52.6 %all-to-all-start = ((bf16[128,16,1024]{0,1,2:T(8,128)(2,1)}), bf16[128,16,1024]{0,1,2:T(8,128)(2,1)}, u32[]{:S(2)}, u32[]{:S(2)}) async-start(bf16[128,16,1024]{0,1,2:T(8,128)(2,1)} %copy.23), calls=%async_computation | async-start | bytes 8388608 | tf_op jit(solution)/shard_map/all_to_all | solution.py:299
  511.9 156.6 %copy-start.1 = (s32[40,2]{0,1:T(2,128)S(1)}, s32[40,2]{0,1:T(2,128)}, u32[]{:S(2)}) copy-start(s32[40,2]{0,1:T(2,128)} %param.3) | copy-start | bytes 964

commit v2 on v1

v2 whole, which is shorter than its diff:
```python
import functools
import math

import jax
import jax.numpy as jnp
from jax import lax
from jax.experimental import pallas as pl
from jax.experimental.pallas import tpu as pltpu
from jax.sharding import PartitionSpec as P

L = 2048
NCH = 512
TAPS = 4
FINE = 64
PAIR = 2
MESH = pl.DeviceIdType.MESH


def filter_window():
    positions = jnp.arange(TAPS * L, dtype=jnp.float32)
    shape_sinc = jnp.sinc((positions - TAPS * L / 2.0) / L)
    tapering = 0.5 - 0.5 * jnp.cos(2.0 * math.pi * positions / (TAPS * L))
    return (shape_sinc * tapering).reshape(TAPS, L)


def turn_angles(rows, samples, quarter):
    channels, parts = rows // 2, rows % 2
    phases = (channels[:, None] * samples[None, :] + quarter * parts[:, None]) % L
    angles = phases.astype(jnp.float32) * (2.0 * math.pi / L)
    return jnp.cos(angles), jnp.sin(angles)


def transform_table():
    rows = jnp.arange(2 * NCH, dtype=jnp.int32)
    coarse_cos, coarse_sin = turn_angles(rows, jnp.arange(L // FINE, dtype=jnp.int32) * FINE, 0)
    fine_cos, fine_sin = turn_angles(rows, jnp.arange(L, dtype=jnp.int32)[:FINE], L // 4)
    spread = lambda values: jnp.repeat(values, FINE, axis=1)
    copied = lambda values: jnp.tile(values, (1, L // FINE))
    return (
        spread(coarse_cos) * copied(fine_cos) - spread(coarse_sin) * copied(fine_sin)
    ).astype(jnp.bfloat16)


def channel_kernel(groups, volt_ref, table_ref, window_ref, out_ref, *scratch):
    extended, filtered, total, load_sem, send_sem, recv_sem = scratch
    width, local_len = volt_ref.shape
    frames = local_len // L
    halo_len = (TAPS - 1) * L
    me = lax.axis_index("chan")
    has_next, has_last = me < groups - 1, me > 0

    load = pltpu.make_async_copy(volt_ref, extended.at[:, pl.ds(0, local_len)], load_sem)
    load.start()
    barrier = pltpu.get_barrier_semaphore()
    for exists, target in ((has_next, me + 1), (has_last, me - 1)):

        @pl.when(exists)
        def _(target=target):
            pl.semaphore_signal(barrier, inc=1, device_id={"chan": target}, device_id_type=MESH)

    pl.semaphore_wait(barrier, has_next.astype(jnp.int32) + has_last.astype(jnp.int32))
    halo = pltpu.make_async_remote_copy(
        src_ref=volt_ref.at[:, pl.ds(0, halo_len)],
        dst_ref=extended.at[:, pl.ds(local_len, halo_len)],
        send_sem=send_sem,
        recv_sem=recv_sem,
        device_id={"chan": me - 1},
        device_id_type=MESH,
    )

    @pl.when(has_last)
    def _():
        halo.start()

    @pl.when(jnp.logical_not(has_next))
    def _():
        extended[:, pl.ds(local_len, halo_len)] = jnp.zeros((width, halo_len), jnp.bfloat16)

    load.wait()
    strip, lanes = 16, 512

    def one_pair(pair):
        for inner in range(PAIR):
            frame = pair * PAIR + inner
            for first in range(0, L, lanes):
                weights = [
                    window_ref[tap : tap + 1, first : first + lanes] for tap in range(TAPS)
                ]

                def one_strip(index, carry):
                    rows = pl.ds(pl.multiple_of(index * strip, strip), strip)
                    value = jnp.zeros((strip, lanes), jnp.float32)
                    for tap in range(TAPS):
                        start = pl.multiple_of((frame + tap) * L + first, 128)
                        value = value + (
                            extended[rows, pl.ds(start, lanes)].astype(jnp.float32) * weights[tap]
                        )
                    to = pl.ds(pl.multiple_of(inner * width + index * strip, strip), strip)
                    filtered[to, first : first + lanes] = value.astype(jnp.bfloat16)
                    return carry

                lax.fori_loop(0, width // strip, one_strip, jnp.int32(0), unroll=2)
        step = min(256, 2 * NCH)
        for row in range(0, 2 * NCH, step):
            product = lax.dot_general(
                table_ref[row : row + step, :],
                filtered[...],
                (((1,), (1,)), ((), ())),
                preferred_element_type=jnp.float32,
            )
            for inner in range(PAIR):
                where = pl.ds(row * frames + pair * PAIR + inner, step, stride=frames)
                total[where, :] = product[:, inner * width : (inner + 1) * width]

    def pairs(first, last):
        def one(pair, carry):
            one_pair(pair)
            return carry

        lax.fori_loop(first, last, one, jnp.int32(0))

    clear = max(0, (frames - TAPS + 1) // PAIR)
    pairs(0, clear)

    @pl.when(has_next)
    def _():
        halo.wait_recv()

    pairs(clear, frames // PAIR)

    def put(index, carry):
        rows = pl.ds(pl.multiple_of(index * 256, 256), 256)
        out_ref[rows, :] = total[rows, :].astype(jnp.bfloat16)
        return carry

    lax.fori_loop(0, out_ref.shape[0] // 256, put, jnp.int32(0))

    @pl.when(has_last)
    def _():
        halo.wait_send()


def channelize(voltages):
    width, local_len = voltages.shape
    frames = local_len // L
    in_vmem = pl.BlockSpec(memory_space=pltpu.VMEM)
    spectra = pl.pallas_call(
        functools.partial(channel_kernel, lax.axis_size("chan")),
        out_shape=jax.ShapeDtypeStruct((2 * NCH * frames, width), jnp.bfloat16),
        in_specs=[pl.BlockSpec(memory_space=pl.ANY), in_vmem, in_vmem],
        out_specs=in_vmem,
        scratch_shapes=[
            pltpu.VMEM((width, local_len + (TAPS - 1) * L), jnp.bfloat16),
            pltpu.VMEM((PAIR * width, L), jnp.bfloat16),
            pltpu.VMEM((2 * NCH * frames, width), jnp.float32),
            pltpu.SemaphoreType.DMA,
            pltpu.SemaphoreType.DMA,
            pltpu.SemaphoreType.DMA,
        ],
        compiler_params=pltpu.CompilerParams(
            collective_id=1, has_side_effects=True, vmem_limit_bytes=56 << 20
        ),
        name="channels",
    )(voltages, transform_table(), filter_window())
    return spectra.reshape(NCH, 2 * frames, width)


def flipped(group, mask, groups):
    result, bit = group, 1
    while bit < groups:
        result = result + (mask // bit % 2) * bit * (1 - 2 * (group // bit % 2))
        bit *= 2
    return result


HALVES = 2


def gather_kernel(sizes, own_ref, all_ref, stage, *sems):
    rows, columns, groups = sizes
    send_line, send_cross, recv_sem, turn_send, turn_recv, local_sem = sems
    channels, depth = own_ref.shape[0] // groups, own_ref.shape[1]
    step = channels // HALVES
    chunks = groups * HALVES
    me, group = lax.axis_index("inp"), lax.axis_index("chan")
    z, x = me // columns, me % columns
    up = ("up", 0, z < rows - 1, me + columns)
    down = ("down", 1, z > 0, me - columns)
    right = ("right", 2, x < columns - 1, me + 1)
    left = ("left", 3, x > 0, me - 1)
    along_z, along_x = (up, down), (right, left)

    barrier = pltpu.get_barrier_semaphore()
    expected = jnp.int32(groups - 1)
    for mask in range(1, groups):
        target = flipped(group, mask, groups)
        pl.semaphore_signal(barrier, inc=1, device_id={"chan": target}, device_id_type=MESH)
    for _, _, exists, target in along_z + along_x:
        expected = expected + exists.astype(jnp.int32)

        @pl.when(exists)
        def _(target=target):
            pl.semaphore_signal(barrier, inc=1, device_id={"inp": target}, device_id_type=MESH)

    pl.semaphore_wait(barrier, expected)

    def part(block, chunk, sender):
        time = flipped(sender, chunk // HALVES, groups)
        return all_ref.at[
            block, pl.ds(chunk % HALVES * step, step), pl.ds(pl.multiple_of(time * depth, depth), depth)
        ]

    def own_part(to, half):
        return own_ref.at[pl.ds(to * channels + half * step, step)]

    def turn(chunk, arriving=False):
        target = flipped(group, chunk // HALVES, groups)
        return pltpu.make_async_remote_copy(
            src_ref=own_part(target, chunk % HALVES),
            dst_ref=part(me, chunk if arriving else chunk % HALVES, group),
            send_sem=turn_send.at[chunk],
            recv_sem=turn_recv.at[chunk],
            device_id={"chan": target},
            device_id_type=MESH,
        )

    def copy(block, chunk, way, to_sems, source=None):
        place = part(block, chunk, group)
        return pltpu.make_async_remote_copy(
            src_ref=place if source is None else source,
            dst_ref=place,
            send_sem=to_sems.at[way[1], block],
            recv_sem=recv_sem.at[block, chunk],
            device_id={"inp": way[3]},
            device_id_type=MESH,
        )

    def send(block, chunk, ways, to_sems, source=None):
        for way in ways:

            @pl.when(way[2])
            def _(way=way):
                copy(block, chunk, way, to_sems, source).start()

    def pass_on(block, chunk, exists, ways, to_sems, origin):
        @pl.when(exists)
        def _():
            copy(block, chunk, origin, to_sems).wait_recv()
            send(block, chunk, ways, to_sems)

    def over(first, last, body):
        def one(chunk, carry):
            body(chunk)
            return carry

        lax.fori_loop(first, last, one, jnp.int32(0))

    over(HALVES, chunks, lambda c: turn(c).start())
    send(me, 0, along_x + along_z, send_cross, own_part(group, 0))
    over(1, HALVES, lambda c: send(me, c, along_z + along_x, send_line, own_part(group, c)))
    load = pltpu.make_async_copy(own_ref.at[pl.ds(group * channels, channels)], stage, local_sem.at[0])
    load.start()
    load.wait()
    store = pltpu.make_async_copy(
        stage,
        all_ref.at[me, :, pl.ds(pl.multiple_of(group * depth, depth), depth)],
        local_sem.at[1],
    )
    store.start()

    def own_turned(mask):
        def one(chunk):
            turn(chunk, True).wait_recv()
            send(me, chunk, along_z + along_x, send_line)

        over(mask * HALVES, (mask + 1) * HALVES, one)

    def line(away, first, last):
        below, above = z >= away, z + away < rows

        def one(chunk):
            pass_on(me - away * columns, chunk, below, along_x + (up,), send_line, down)
            pass_on(me + away * columns, chunk, above, along_x + (down,), send_line, up)

        over(first, last, one)

    def crossing(away):
        below, above = z >= away, z + away < rows
        for column in range(columns):
            low = (z - away) * columns + column
            high = (z + away) * columns + column
            pass_on(low, 0, below, (up,), send_cross, down)
            pass_on(high, 0, above, (down,), send_cross, up)

    for away in range(1, columns):
        pass_on(me - away, 0, x >= away, (right,) + along_z, send_cross, left)
        pass_on(me + away, 0, x + away < columns, (left,) + along_z, send_cross, right)
    own_turned(1)
    crossing(1)
    line(1, 1, HALVES)
    for mask in range(2, groups):
        own_turned(mask)
        line(1, (mask - 1) * HALVES, mask * HALVES)
    line(1, chunks - HALVES, chunks)
    for away in range(2, rows):
        crossing(away)
        line(away, 1, chunks)
    for away in range(1, columns):
        for row in range(rows):
            before = row * columns + x - away
            after = row * columns + x + away

            def across(chunk):
                pass_on(before, chunk, x >= away, (right,), send_line, left)
                pass_on(after, chunk, x + away < columns, (left,), send_line, right)

            over(1, chunks, across)

    def drain(block, way, cond, to_sems, count):
        @pl.when(jnp.logical_and(cond, way[2]))
        def _():
            whole = all_ref.at[block, pl.ds(0, count * (channels // chunks))]
            pltpu.make_async_remote_copy(
                src_ref=whole,
                dst_ref=whole,
                send_sem=to_sems.at[way[1], block],
                recv_sem=recv_sem.at[block, 0],
                device_id={"inp": way[3]},
                device_id_type=MESH,
            ).wait_send()

    for row in range(rows):
        for column in range(columns):
            block = row * columns + column
            here, same = x == column, z == row
            drain(block, up, jnp.logical_and(here, z >= row), send_line, chunks - 1)
            drain(block, down, jnp.logical_and(here, z <= row), send_line, chunks - 1)
            drain(block, right, x >= column, send_line, chunks - 1)
            drain(block, left, x <= column, send_line, chunks - 1)
            drain(block, up, z >= row, send_cross, 1)
            drain(block, down, z <= row, send_cross, 1)
            drain(block, right, jnp.logical_and(same, x >= column), send_cross, 1)
            drain(block, left, jnp.logical_and(same, x <= column), send_cross, 1)
    over(HALVES, chunks, lambda c: turn(c).wait_send())
    store.wait()


def gather(spectra):
    devices, groups = lax.axis_size("inp"), lax.axis_size("chan")
    columns = 1 << (int(math.log2(devices)) // 2)
    rows = devices // columns
    channels, depth, width = spectra.shape[0] // groups, spectra.shape[1], spectra.shape[2]
    chunks = groups * HALVES
    return pl.pallas_call(
        functools.partial(gather_kernel, (rows, columns, groups)),
        out_shape=jax.ShapeDtypeStruct((devices, channels, groups * depth, width), spectra.dtype),
        in_specs=[pl.BlockSpec(memory_space=pl.ANY)],
        out_specs=pl.BlockSpec(memory_space=pl.ANY),
        scratch_shapes=[
            pltpu.VMEM((channels, depth, width), spectra.dtype),
            pltpu.SemaphoreType.DMA((4, devices)),
            pltpu.SemaphoreType.DMA((4, devices)),
            pltpu.SemaphoreType.DMA((devices, chunks)),
            pltpu.SemaphoreType.DMA((chunks,)),
            pltpu.SemaphoreType.DMA((chunks,)),
            pltpu.SemaphoreType.DMA((2,)),
        ],
        compiler_params=pltpu.CompilerParams(collective_id=0, has_side_effects=True),
        name="gather",
    )(spectra)


def tile_kernel(slots, frames, groups, table_ref, all_ref, out_ref):
    depth = all_ref.shape[2]
    local = depth // (2 * groups)

    def scaled(block, channel):
        rows = all_ref[block, channel].astype(jnp.float32)
        autopower = jnp.sum(rows * rows, axis=0, keepdims=True) / frames + 1e-06
        return rows * (1.0 / (math.sqrt(frames) * jnp.sqrt(autopower)))

    def one(channel, carry):
        for slot in range(slots):
            first, second = table_ref[slot, 0], table_ref[slot, 1]
            left = scaled(jnp.maximum(first, 0), channel)
            left = jnp.where(first >= 0, left, jnp.zeros_like(left)).astype(jnp.bfloat16)
            right = scaled(jnp.maximum(second, 0), channel).astype(jnp.bfloat16)
            pieces = []
            for start in range(0, depth, 2 * local):
                pieces.append(-right[start + local : start + 2 * local])
                pieces.append(right[start : start + local])
            partner = jnp.concatenate([right, jnp.concatenate(pieces, axis=0)], axis=1)
            out_ref[channel, slot] = lax.dot_general(
                left, partner, (((0,), (0,)), ((), ())), preferred_element_type=jnp.float32
            )
        return carry

    lax.fori_loop(0, all_ref.shape[1], one, jnp.int32(0), unroll=2)


def make_tiles(everything, slot_rows):
    devices, channel_count, depth, width = everything.shape
    slots = slot_rows.shape[0]
    group = 8
    return pl.pallas_call(
        functools.partial(tile_kernel, slots, depth // 2, lax.axis_size("chan")),
        out_shape=jax.ShapeDtypeStruct((channel_count, slots, width, 2 * width), jnp.float32),
        grid_spec=pltpu.PrefetchScalarGridSpec(
            num_scalar_prefetch=1,
            grid=(channel_count // group,),
            in_specs=[pl.BlockSpec((devices, group, depth, width), lambda c, t: (0, c, 0, 0))],
            out_specs=pl.BlockSpec((group, slots, width, 2 * width), lambda c, t: (c, 0, 0, 0)),
        ),
        compiler_params=pltpu.CompilerParams(vmem_limit_bytes=56 << 20),
        name="tiles",
    )(slot_rows, everything)


def on_device(voltages, tile_table):
    everything = gather(channelize(voltages))
    slot_total = tile_table.shape[0] // lax.axis_size("inp")
    slot_rows = lax.dynamic_slice_in_dim(
        tile_table, lax.axis_index("inp") * slot_total, slot_total, 0
    )
    return make_tiles(everything, slot_rows)


def solution(mesh):
    placed = (P("inp", "chan"), P())
    return jax.shard_map(
        on_device,
        mesh=mesh,
        in_specs=placed,
        out_specs=P("chan", "inp", None, None),
        check_vma=False,
    )
```

time: 670 us -> 428 us (0.64)
  the two profiles are of different devices: /device:TPU:9 before, /device:TPU:0 now
where the time goes in v2:
time: 428 us; the launch traced here: 427 us
  Pallas kernels  413 us (96%)
  local copies, waits for them, and re-layouts  7.9 us (2%)
  other arithmetic  6.26 us (1%)
    pallas_call x1, Pallas kernels, gather(): pl.pallas_call(functools.partial(gather_kernel, (rows, columns, groups)),...  337 us
    pallas_call x1, Pallas kernels, make_tiles(): pl.pallas_call(functools.partial(tile_kernel, slots, depth // 2, lax.axis...  46.9 us
    pallas_call x1, Pallas kernels, channelize(): pl.pallas_call(functools.partial(channel_kernel, lax.axis_size('chan')),...  29 us

profile of v2, /device:TPU:0, one launch (start us, length us, event | category | flops | bytes accessed | tf_op | source)
XLA Modules:
  0.0 426.8 jit_solution(5182519126804049914)
XLA Ops:
  0.0 0.0 copy-start
  0.0 0.7 copy-done
  0.7 0.1 constant_dynamic-slice_fusion
  0.8 0.7 copy.6.table_ref
  1.4 0.9 fusion.15.window_ref
  2.4 0.6 fusion.9
  3.0 1.1 fusion.4
  4.1 3.6 subtract_convert_fusion
  7.7 6.5 %copy.5.table_ref = bf16[1024,2048]{1,0:T(8,128)(2,1)} copy(bf16[1024,2048]{0,1:T(8,128)(2,1)} %bitcast.2) | data formatting | bytes 8388608 | tf_op jit(solution)/shard_map/convert_element_type | solution.py:41
  14.2 29.0 %channels.1 = bf16[16384,128]{1,0:T(8,128)(2,1)} custom-call(bf16[128,32768]{1,0:T(8,128)(2,1)} %volt_ref.1, bf16[1024,2048]{1,0:T(8,128)(2,1)} %copy.5.table_ref, f32[4,2048]{1,0:T(4,128)} %fusion.15.window_ref), custom_call_target="tpu_custom_call" | custom-call | tf_op jit(solution)/shard_map/channels/pallas_call | solution.py:147
  43.2 336.7 %gather.1.all_ref = bf16[8,128,128,128]{3,2,1,0:T(8,128)(2,1)} custom-call(bf16[512,32,128]{2,1,0:T(8,128)(2,1)} %bitcast.3), custom_call_target="tpu_custom_call" | custom-call | tf_op jit(solution)/shard_map/gather/pallas_call | solution.py:354
  379.9 46.9 %tiles.1 = f32[128,5,128,256]{3,2,1,0:T(8,128)} custom-call(s32[5,2]{1,0:T(8,128)} %copy.6.table_ref, bf16[8,128,128,128]{3,2,1,0:T(8,128)(2,1)} %gather.1.all_ref), custom_call_target="tpu_custom_call" | custom-call | tf_op jit(solution)/shard_map/tiles/pallas_call | solution.py:405
  (3 shorter events, 0.0 us)
Async XLA Ops:
  0.0 0.7 copy-start

commit v3 on v2

--- a/solution.py
+++ b/solution.py
@@ -11,7 +11,7 @@
 L = 2048
 NCH = 512
 TAPS = 4
-FINE = 64
+FINE = 128
 PAIR = 2
 MESH = pl.DeviceIdType.MESH
 
@@ -30,19 +30,33 @@
     return jnp.cos(angles), jnp.sin(angles)
 
 
-def transform_table():
+def table_factors():
     rows = jnp.arange(2 * NCH, dtype=jnp.int32)
-    coarse_cos, coarse_sin = turn_angles(rows, jnp.arange(L // FINE, dtype=jnp.int32) * FINE, 0)
-    fine_cos, fine_sin = turn_angles(rows, jnp.arange(L, dtype=jnp.int32)[:FINE], L // 4)
-    spread = lambda values: jnp.repeat(values, FINE, axis=1)
-    copied = lambda values: jnp.tile(values, (1, L // FINE))
-    return (
-        spread(coarse_cos) * copied(fine_cos) - spread(coarse_sin) * copied(fine_sin)
-    ).astype(jnp.bfloat16)
-
-
-def channel_kernel(groups, volt_ref, table_ref, window_ref, out_ref, *scratch):
-    extended, filtered, total, load_sem, send_sem, recv_sem = scratch
+    coarse = turn_angles(rows, jnp.arange(L // FINE, dtype=jnp.int32) * FINE, 0)
+    fine = turn_angles(rows, jnp.arange(L, dtype=jnp.int32)[:FINE], L // 4)
+    return coarse + fine
+
+
+def fill_table(factors, table):
+    coarse_cos, coarse_sin, fine_cos, fine_sin = factors
+    strip = 128
+
+    def one(index, carry):
+        rows = pl.ds(pl.multiple_of(index * strip, strip), strip)
+        cosines, sines = fine_cos[rows, :], fine_sin[rows, :]
+        for column in range(L // FINE):
+            table[rows, column * FINE : (column + 1) * FINE] = (
+                coarse_cos[rows, column : column + 1] * cosines
+                - coarse_sin[rows, column : column + 1] * sines
+            ).astype(jnp.bfloat16)
+        return carry
+
+    lax.fori_loop(0, table.shape[0] // strip, one, jnp.int32(0))
+
+
+def channel_kernel(groups, volt_ref, *refs):
+    factors, window_ref, out_ref, scratch = refs[:4], refs[4], refs[5], refs[6:]
+    extended, filtered, table_ref, total, load_sem, send_sem, recv_sem = scratch
     width, local_len = volt_ref.shape
     frames = local_len // L
     halo_len = (TAPS - 1) * L
@@ -76,6 +90,7 @@
     def _():
         extended[:, pl.ds(local_len, halo_len)] = jnp.zeros((width, halo_len), jnp.bfloat16)
 
+    fill_table(factors, table_ref)
     load.wait()
     strip, lanes = 16, 512
 
@@ -147,11 +162,12 @@
     spectra = pl.pallas_call(
         functools.partial(channel_kernel, lax.axis_size("chan")),
         out_shape=jax.ShapeDtypeStruct((2 * NCH * frames, width), jnp.bfloat16),
-        in_specs=[pl.BlockSpec(memory_space=pl.ANY), in_vmem, in_vmem],
+        in_specs=[pl.BlockSpec(memory_space=pl.ANY)] + [in_vmem] * 5,
         out_specs=in_vmem,
         scratch_shapes=[
             pltpu.VMEM((width, local_len + (TAPS - 1) * L), jnp.bfloat16),
             pltpu.VMEM((PAIR * width, L), jnp.bfloat16),
+            pltpu.VMEM((2 * NCH, L), jnp.bfloat16),
             pltpu.VMEM((2 * NCH * frames, width), jnp.float32),
             pltpu.SemaphoreType.DMA,
             pltpu.SemaphoreType.DMA,
@@ -161,7 +177,7 @@
             collective_id=1, has_side_effects=True, vmem_limit_bytes=56 << 20
         ),
         name="channels",
-    )(voltages, transform_table(), filter_window())
+    )(voltages, *table_factors(), filter_window())
     return spectra.reshape(NCH, 2 * frames, width)
 
 
@@ -173,15 +189,15 @@
     return result
 
 
-HALVES = 2
+PARTS = 4
 
 
 def gather_kernel(sizes, own_ref, all_ref, stage, *sems):
-    rows, columns, groups = sizes
+    rows, columns, groups, crossed = sizes
     send_line, send_cross, recv_sem, turn_send, turn_recv, local_sem = sems
     channels, depth = own_ref.shape[0] // groups, own_ref.shape[1]
-    step = channels // HALVES
-    chunks = groups * HALVES
+    step = channels // PARTS
+    chunks = 2 + (groups - 1) * PARTS
     me, group = lax.axis_index("inp"), lax.axis_index("chan")
     z, x = me // columns, me % columns
     up = ("up", 0, z < rows - 1, me + columns)
@@ -204,28 +220,37 @@
 
     pl.semaphore_wait(barrier, expected)
 
-    def part(block, chunk, sender):
-        time = flipped(sender, chunk // HALVES, groups)
+    def where(chunk):
+        if isinstance(chunk, int) and chunk < 2:
+            return 0, chunk * crossed, (channels - crossed if chunk else crossed)
+        return 1 + (chunk - 2) // PARTS, (chunk - 2) % PARTS * step, step
+
+    def rows_of(block, first, count, time):
         return all_ref.at[
-            block, pl.ds(chunk % HALVES * step, step), pl.ds(pl.multiple_of(time * depth, depth), depth)
+            block, pl.ds(first, count), pl.ds(pl.multiple_of(time * depth, depth), depth)
         ]
 
-    def own_part(to, half):
-        return own_ref.at[pl.ds(to * channels + half * step, step)]
+    def part(block, chunk):
+        mask, first, count = where(chunk)
+        return rows_of(block, first, count, flipped(group, mask, groups))
+
+    def own_part(chunk):
+        mask, first, count = where(chunk)
+        return own_ref.at[pl.ds(flipped(group, mask, groups) * channels + first, count)]
 
     def turn(chunk, arriving=False):
-        target = flipped(group, chunk // HALVES, groups)
+        mask, first, count = where(chunk)
         return pltpu.make_async_remote_copy(
-            src_ref=own_part(target, chunk % HALVES),
-            dst_ref=part(me, chunk if arriving else chunk % HALVES, group),
+            src_ref=own_part(chunk),
+            dst_ref=part(me, chunk) if arriving else rows_of(me, first, count, group),
             send_sem=turn_send.at[chunk],
             recv_sem=turn_recv.at[chunk],
-            device_id={"chan": target},
+            device_id={"chan": flipped(group, mask, groups)},
             device_id_type=MESH,
         )
 
     def copy(block, chunk, way, to_sems, source=None):
-        place = part(block, chunk, group)
+        place = part(block, chunk)
         return pltpu.make_async_remote_copy(
             src_ref=place if source is None else source,
             dst_ref=place,
@@ -253,11 +278,17 @@
             body(chunk)
             return carry
 
-        lax.fori_loop(first, last, one, jnp.int32(0))
-
-    over(HALVES, chunks, lambda c: turn(c).start())
-    send(me, 0, along_x + along_z, send_cross, own_part(group, 0))
-    over(1, HALVES, lambda c: send(me, c, along_z + along_x, send_line, own_part(group, c)))
+        for chunk in range(first, min(last, 2)):
+            body(chunk)
+        if last > 2:
+            lax.fori_loop(max(first, 2), last, one, jnp.int32(0))
+
+    def of_mask(mask):
+        return (1, 2) if mask == 0 else (2 + (mask - 1) * PARTS, 2 + mask * PARTS)
+
+    over(2, chunks, lambda c: turn(c).start())
+    send(me, 0, along_x + along_z, send_cross, own_part(0))
+    send(me, 1, along_z + along_x, send_line, own_part(1))
     load = pltpu.make_async_copy(own_ref.at[pl.ds(group * channels, channels)], stage, local_sem.at[0])
     load.start()
     load.wait()
@@ -273,7 +304,7 @@
             turn(chunk, True).wait_recv()
             send(me, chunk, along_z + along_x, send_line)
 
-        over(mask * HALVES, (mask + 1) * HALVES, one)
+        over(*of_mask(mask), one)
 
     def line(away, first, last):
         below, above = z >= away, z + away < rows
@@ -297,11 +328,11 @@
         pass_on(me + away, 0, x + away < columns, (left,) + along_z, send_cross, right)
     own_turned(1)
     crossing(1)
-    line(1, 1, HALVES)
+    line(1, *of_mask(0))
     for mask in range(2, groups):
         own_turned(mask)
-        line(1, (mask - 1) * HALVES, mask * HALVES)
-    line(1, chunks - HALVES, chunks)
+        line(1, *of_mask(mask - 1))
+    line(1, *of_mask(groups - 1))
     for away in range(2, rows):
         crossing(away)
         line(away, 1, chunks)
@@ -319,7 +350,7 @@
     def drain(block, way, cond, to_sems, count):
         @pl.when(jnp.logical_and(cond, way[2]))
         def _():
-            whole = all_ref.at[block, pl.ds(0, count * (channels // chunks))]
+            whole = all_ref.at[block, pl.ds(0, count)]
             pltpu.make_async_remote_copy(
                 src_ref=whole,
                 dst_ref=whole,
@@ -333,15 +364,15 @@
         for column in range(columns):
             block = row * columns + column
             here, same = x == column, z == row
-            drain(block, up, jnp.logical_and(here, z >= row), send_line, chunks - 1)
-            drain(block, down, jnp.logical_and(here, z <= row), send_line, chunks - 1)
-            drain(block, right, x >= column, send_line, chunks - 1)
-            drain(block, left, x <= column, send_line, chunks - 1)
-            drain(block, up, z >= row, send_cross, 1)
-            drain(block, down, z <= row, send_cross, 1)
-            drain(block, right, jnp.logical_and(same, x >= column), send_cross, 1)
-            drain(block, left, jnp.logical_and(same, x <= column), send_cross, 1)
-    over(HALVES, chunks, lambda c: turn(c).wait_send())
+            drain(block, up, jnp.logical_and(here, z >= row), send_line, channels - crossed // groups)
+            drain(block, down, jnp.logical_and(here, z <= row), send_line, channels - crossed // groups)
+            drain(block, right, x >= column, send_line, channels - crossed // groups)
+            drain(block, left, x <= column, send_line, channels - crossed // groups)
+            drain(block, up, z >= row, send_cross, crossed // groups)
+            drain(block, down, z <= row, send_cross, crossed // groups)
+            drain(block, right, jnp.logical_and(same, x >= column), send_cross, crossed // groups)
+            drain(block, left, jnp.logical_and(same, x <= column), send_cross, crossed // groups)
+    over(2, chunks, lambda c: turn(c).wait_send())
     store.wait()
 
 
@@ -350,9 +381,11 @@
     columns = 1 << (int(math.log2(devices)) // 2)
     rows = devices // columns
     channels, depth, width = spectra.shape[0] // groups, spectra.shape[1], spectra.shape[2]
-    chunks = groups * HALVES
+    chunks = 2 + (groups - 1) * PARTS
+    share = ((columns - 1) * rows - rows + 1) / (2 * (rows - 1) * (columns - 1))
+    crossed = min(int(0.94 * share * groups * channels), channels - 16) // 16 * 16
     return pl.pallas_call(
-        functools.partial(gather_kernel, (rows, columns, groups)),
+        functools.partial(gather_kernel, (rows, columns, groups, crossed)),
         out_shape=jax.ShapeDtypeStruct((devices, channels, groups * depth, width), spectra.dtype),
         in_specs=[pl.BlockSpec(memory_space=pl.ANY)],
         out_specs=pl.BlockSpec(memory_space=pl.ANY),
@@ -365,7 +398,9 @@
             pltpu.SemaphoreType.DMA((chunks,)),
             pltpu.SemaphoreType.DMA((2,)),
         ],
-        compiler_params=pltpu.CompilerParams(collective_id=0, has_side_effects=True),
+        compiler_params=pltpu.CompilerParams(
+            collective_id=0, has_side_effects=True, vmem_limit_bytes=4 << 20
+        ),
         name="gather",
     )(spectra)
 
@@ -411,7 +446,7 @@
             in_specs=[pl.BlockSpec((devices, group, depth, width), lambda c, t: (0, c, 0, 0))],
             out_specs=pl.BlockSpec((group, slots, width, 2 * width), lambda c, t: (c, 0, 0, 0)),
         ),
-        compiler_params=pltpu.CompilerParams(vmem_limit_bytes=56 << 20),
+        compiler_params=pltpu.CompilerParams(vmem_limit_bytes=24 << 20),
         name="tiles",
     )(slot_rows, everything)
 

time: 428 us -> 430 us (level)
  local copies, waits for them, and re-layouts: 7.9 us -> 14.3 us
  Pallas kernels: 413 us -> 407 us
    unnamed x3 -> x7, local copies, waits for them, and re-layouts: 1.35 us -> 14 us
    pallas_call x1, Pallas kernels: 337 us -> 330 us  [gather(): pl.pallas_call(functools.partial(gather_kernel, (rows, columns, groups, c...]
    sin x0 -> x2, other arithmetic: none -> 6.34 us  [turn_angles(): return (jnp.cos(angles), jnp.sin(angles))]
    convert_element_type x1, local copies, waits for them, and re-layouts: 6.47 us -> 0.19 us  [turn_angles(): angles = phases.astype(jnp.float32) * (2.0 * math.pi / L)]
where the time goes in v3:
time: 430 us; the launch traced here: 429 us
  Pallas kernels  407 us (95%)
  local copies, waits for them, and re-layouts  14.3 us (3%)
  other arithmetic  7.38 us (2%)
    pallas_call x1, Pallas kernels, gather(): pl.pallas_call(functools.partial(gather_kernel, (rows, columns, groups, c...  330 us
    pallas_call x1, Pallas kernels, make_tiles(): pl.pallas_call(functools.partial(tile_kernel, slots, depth // 2, lax.axis...  46.8 us
    pallas_call x1, Pallas kernels, channelize(): pl.pallas_call(functools.partial(channel_kernel, lax.axis_size('chan')),...  30.4 us
    unnamed x7, local copies, waits for them, and re-layouts  14 us

profile of v3, /device:TPU:0, one launch (start us, length us, event | category | flops | bytes accessed | tf_op | source)
XLA Modules:
  0.0 429.0 jit_solution(17968255928362353378)
XLA Ops:
  0.0 0.0 copy-start
  0.0 0.7 copy-done
  0.7 0.1 constant_dynamic-slice_fusion
  0.8 0.1 copy.6.table_ref
  0.9 0.9 fusion.12.refs_4_
  1.8 0.1 fusion.5
  1.9 0.2 copy.5
  2.1 2.7 multiply_sine_fusion
  4.8 3.6 fusion.3
  8.4 30.4 %channels.1 = bf16[16384,128]{1,0:T(8,128)(2,1)} custom-call(bf16[128,32768]{1,0:T(8,128)(2,1)} %volt_ref.1, f32[1024,16]{1,0:T(8,128)} %get-tuple-element.6.refs_0_, f32[1024,16]{1,0:T(8,128)} %get-tuple-element.5.refs_1_, f32[1024,128]{1,0:T(8,128)} %get-tuple-element.8.refs_2_, f32[1024,128]{1,0:T(8,128)} %get-tuple-element.7.refs_3_, ...), custom_call_target="tpu_custom_call" | custom-call | tf_op jit(solution)/shard_map/channels/pallas_call | solution.py:162
  38.9 0.0 copy-start.2
  38.9 2.2 copy-done.2
  41.1 330.1 %gather.1.all_ref = bf16[8,128,128,128]{3,2,1,0:T(8,128)(2,1)S(1)} custom-call(bf16[512,32,128]{2,1,0:T(8,128)(2,1)S(1)} %bitcast.1), custom_call_target="tpu_custom_call" | custom-call | tf_op jit(solution)/shard_map/gather/pallas_call | solution.py:387
  371.2 0.0 copy-start.1
  371.2 11.1 %copy-done.1 = bf16[8,128,128,128]{3,2,1,0:T(8,128)(2,1)} copy-done((bf16[8,128,128,128]{3,2,1,0:T(8,128)(2,1)}, bf16[8,128,128,128]{3,2,1,0:T(8,128)(2,1)S(1)}, u32[]{:S(2)}) %copy-start.1) | copy-done | bytes 33554456
  382.2 46.8 %tiles.1 = f32[128,5,128,256]{3,2,1,0:T(8,128)} custom-call(s32[5,2]{1,0:T(8,128)S(1)} %copy.6.table_ref, bf16[8,128,128,128]{3,2,1,0:T(8,128)(2,1)} %copy-done.1), custom_call_target="tpu_custom_call" | custom-call | tf_op jit(solution)/shard_map/tiles/pallas_call | solution.py:440
  (3 shorter events, 0.0 us)
Async XLA Ops:
  0.0 0.7 copy-start
  38.9 2.2 copy-start.2
  371.2 11.1 %copy-start.1 = (bf16[8,128,128,128]{3,2,1,0:T(8,128)(2,1)}, bf16[8,128,128,128]{3,2,1,0:T(8,128)(2,1)S(1)}, u32[]{:S(2)}) copy-start(bf16[8,128,128,128]{3,2,1,0:T(8,128)(2,1)S(1)} %gather.1.all_ref) | copy-start | bytes 100663296

commit v4 on v3

--- a/solution.py
+++ b/solution.py
@@ -189,7 +189,7 @@
     return result
 
 
-PARTS = 4
+PARTS = 2
 
 
 def gather_kernel(sizes, own_ref, all_ref, stage, *sems):
@@ -436,7 +436,11 @@
 def make_tiles(everything, slot_rows):
     devices, channel_count, depth, width = everything.shape
     slots = slot_rows.shape[0]
+    lanes = max(width, 128)
+    block_bytes = 2 * devices * depth * lanes + 4 * slots * width * max(2 * width, 128)
     group = 8
+    while 2 * group * block_bytes > 16 << 20:
+        group //= 2
     return pl.pallas_call(
         functools.partial(tile_kernel, slots, depth // 2, lax.axis_size("chan")),
         out_shape=jax.ShapeDtypeStruct((channel_count, slots, width, 2 * width), jnp.float32),
@@ -446,7 +450,7 @@
             in_specs=[pl.BlockSpec((devices, group, depth, width), lambda c, t: (0, c, 0, 0))],
             out_specs=pl.BlockSpec((group, slots, width, 2 * width), lambda c, t: (c, 0, 0, 0)),
         ),
-        compiler_params=pltpu.CompilerParams(vmem_limit_bytes=24 << 20),
+        compiler_params=pltpu.CompilerParams(vmem_limit_bytes=20 << 20),
         name="tiles",
     )(slot_rows, everything)
 

time: 430 us -> 416 us (0.967)
  local copies, waits for them, and re-layouts: 14.3 us -> 3.22 us
    unnamed x7 -> x5, local copies, waits for them, and re-layouts: 14 us -> 2.95 us
    pallas_call x1, Pallas kernels: 46.8 us -> 39.4 us  [make_tiles(): pl.pallas_call(functools.partial(tile_kernel, slots, depth // 2, lax.axis...]
    pallas_call x1, Pallas kernels: 330 us -> 335 us  [gather(): pl.pallas_call(functools.partial(gather_kernel, (rows, columns, groups, c...]
where the time goes in v4:
time: 416 us
  Pallas kernels  405 us (97%)
  other arithmetic  7.41 us (2%)
    pallas_call x1, Pallas kernels, gather(): pl.pallas_call(functools.partial(gather_kernel, (rows, columns, groups, c...  335 us
    pallas_call x1, Pallas kernels, make_tiles(): pl.pallas_call(functools.partial(tile_kernel, slots, depth // 2, lax.axis...  39.4 us
    pallas_call x1, Pallas kernels, channelize(): pl.pallas_call(functools.partial(channel_kernel, lax.axis_size('chan')),...  30.4 us

profile of v4, /device:TPU:0, one launch (start us, length us, event | category | flops | bytes accessed | tf_op | source)
XLA Modules:
  0.0 415.5 jit_solution(4940947454934622775)
XLA Ops:
  0.0 0.0 copy-start
  0.0 0.7 copy-done
  0.7 0.1 constant_dynamic-slice_fusion
  0.8 0.1 copy.6.table_ref
  0.9 0.9 fusion.12.refs_4_
  1.8 0.1 fusion.5
  1.9 0.2 copy.5
  2.1 2.8 multiply_sine_fusion
  4.9 3.6 fusion.3
  8.5 30.4 %channels.1 = bf16[16384,128]{1,0:T(8,128)(2,1)} custom-call(bf16[128,32768]{1,0:T(8,128)(2,1)} %volt_ref.1, f32[1024,16]{1,0:T(8,128)} %get-tuple-element.6.refs_0_, f32[1024,16]{1,0:T(8,128)} %get-tuple-element.5.refs_1_, f32[1024,128]{1,0:T(8,128)} %get-tuple-element.8.refs_2_, f32[1024,128]{1,0:T(8,128)} %get-tuple-element.7.refs_3_, ...), custom_call_target="tpu_custom_call" | custom-call | tf_op jit(solution)/shard_map/channels/pallas_call | solution.py:162
  38.9 0.0 copy-start.1
  38.9 2.2 copy-done.1
  41.1 335.1 %gather.1.all_ref = bf16[8,128,128,128]{3,2,1,0:T(8,128)(2,1)S(1)} custom-call(bf16[512,32,128]{2,1,0:T(8,128)(2,1)S(1)} %bitcast.1), custom_call_target="tpu_custom_call" | custom-call | tf_op jit(solution)/shard_map/gather/pallas_call | solution.py:387
  376.1 39.4 %tiles.1 = f32[128,5,128,256]{3,2,1,0:T(8,128)} custom-call(s32[5,2]{1,0:T(8,128)S(1)} %copy.6.table_ref, bf16[8,128,128,128]{3,2,1,0:T(8,128)(2,1)S(1)} %gather.1.all_ref), custom_call_target="tpu_custom_call" | custom-call | tf_op jit(solution)/shard_map/tiles/pallas_call | solution.py:444
  (3 shorter events, 0.0 us)
Async XLA Ops:
  0.0 0.7 copy-start
  38.9 2.2 copy-start.1
